TPU v7x, 256 devices: a whole 4x4x8 slice. The times are simulated.
256 devices in a mesh: seq: 32 (over z, y), head: 8 (over x, core).
Axes of the slice: x: 4, y: 4, z: 8, core: 2. Of those that a mesh axis runs over, the one named last changes fastest.
Arguments:
- query: bfloat16 [16384, 6144], P('seq', 'head'), may hold values from -6 to 6
- key: bfloat16 [16384, 6144], P('seq', 'head'), may hold values from -6 to 6
- value: bfloat16 [16384, 6144], P('seq', 'head'), may hold values from -6 to 6
- init_state: float32 [48, 128, 128], P('head'), may hold values from -768 to 768
- out_weight: bfloat16 [6144, 6144], P(('head', 'seq')), may hold values from -0.078125 to 0.078125
- out_grad: bfloat16 [16384, 6144], P('seq'), may hold values from -24 to 24
Outputs:
- mixed: bfloat16 [16384, 6144], P('seq', 'head')
- grad_query: bfloat16 [16384, 6144], P('seq', 'head')
- grad_key: bfloat16 [16384, 6144], P('seq', 'head')
- grad_value: bfloat16 [16384, 6144], P('seq', 'head')
- init_grad: float32 [48, 128, 128], P('head')
All inputs are finite; a program needn't handle non-finite values.
Results may differ from a plain program's by a relative error of at most 0.017.
Values may be sent and summed in bfloat16 or wider, within the bound.
A program may use at most 128 MiB of HBM per device.

v0:
```python
import jax
import jax.numpy as jnp
from jax import lax
from jax.sharding import PartitionSpec as P

EPS = 1e-06


def prefix(value, axis, join, neutral, backward):
    count = lax.axis_size(axis)
    place = lax.axis_index(axis)
    ahead = count - 1 - place if backward else place
    gathered = lax.all_gather(value.astype(jnp.bfloat16), axis)
    state = jnp.zeros_like(value) + jnp.asarray(neutral, value.dtype)

    def one(turn, state):
        source = count - 1 - turn if backward else turn
        return join(state, lax.dynamic_index_in_dim(gathered, source, 0, False).astype(value.dtype))

    return lax.fori_loop(0, ahead, one, state)


def normalize(attended):
    return attended * lax.rsqrt(jnp.mean(attended * attended, axis=-1, keepdims=True) + EPS)


def add_states(earlier, later):
    return earlier + later


def shards(query, key, value, init_state, out_weight, out_grad):
    tok_rows = query.shape[0]
    width = query.shape[1]
    heads_here = init_state.shape[0]
    head_dim = init_state.shape[2]
    queries = query.reshape(tok_rows, heads_here, head_dim)
    key_rows = key.reshape(tok_rows, heads_here, head_dim)
    val_rows = value.reshape(tok_rows, heads_here, head_dim)
    local_state = jnp.einsum("thi,thj->hij", key_rows, val_rows, preferred_element_type=jnp.float32)
    zero_state = jnp.zeros_like(local_state)
    earlier = prefix(local_state, "seq", add_states, zero_state, False)
    state_half = (init_state + earlier).astype(jnp.bfloat16)
    row_index = lax.broadcasted_iota(jnp.int32, (tok_rows, tok_rows), 0)
    col_index = lax.broadcasted_iota(jnp.int32, (tok_rows, tok_rows), 1)
    causal = col_index <= row_index
    scores = jnp.einsum("thi,shi->hts", queries, key_rows, preferred_element_type=jnp.float32)
    attn_weights = jnp.where(causal, scores, 0.0).astype(jnp.bfloat16)
    attended = jnp.einsum(
        "hts,shj->thj", attn_weights, val_rows, preferred_element_type=jnp.float32
    )
    attended = attended + jnp.einsum(
        "thi,hij->thj", queries, state_half, preferred_element_type=jnp.float32
    )
    normed = normalize(attended).astype(jnp.bfloat16).reshape(tok_rows, width)
    weight_rows = lax.all_gather(out_weight, "seq", axis=0, tiled=True)
    projected = jnp.dot(normed, weight_rows, preferred_element_type=jnp.float32)
    grad_normed = lax.dot_general(
        out_grad, weight_rows, (((1,), (1,)), ((), ())), preferred_element_type=jnp.float32
    )
    mixed = lax.psum_scatter(
        projected.astype(jnp.bfloat16), "head", scatter_dimension=1, tiled=True
    )
    _, norm_back = jax.vjp(normalize, attended)
    grad_att = norm_back(grad_normed.reshape(tok_rows, heads_here, head_dim))[0].astype(
        jnp.bfloat16
    )
    grad_scores = jnp.einsum("thj,shj->hts", grad_att, val_rows, preferred_element_type=jnp.float32)
    grad_scores = jnp.where(causal, grad_scores, 0.0).astype(jnp.bfloat16)
    own_adjoint = jnp.einsum("thi,thj->hij", queries, grad_att, preferred_element_type=jnp.float32)
    later = prefix(own_adjoint, "seq", add_states, zero_state, True)
    later_half = later.astype(jnp.bfloat16)
    grad_query = jnp.einsum(
        "hts,shi->thi", grad_scores, key_rows, preferred_element_type=jnp.float32
    )
    grad_query = grad_query + jnp.einsum(
        "thj,hij->thi", grad_att, state_half, preferred_element_type=jnp.float32
    )
    grad_key = jnp.einsum("hts,thi->shi", grad_scores, queries, preferred_element_type=jnp.float32)
    grad_key = grad_key + jnp.einsum(
        "thj,hij->thi", val_rows, later_half, preferred_element_type=jnp.float32
    )
    grad_value = jnp.einsum(
        "hts,thj->shj", attn_weights, grad_att, preferred_element_type=jnp.float32
    )
    grad_value = grad_value + jnp.einsum(
        "thi,hij->thj", key_rows, later_half, preferred_element_type=jnp.float32
    )
    init_grad = lax.psum(own_adjoint.astype(jnp.bfloat16), "seq").astype(jnp.float32)
    return (
        mixed,
        grad_query.reshape(tok_rows, width).astype(jnp.bfloat16),
        grad_key.reshape(tok_rows, width).astype(jnp.bfloat16),
        grad_value.reshape(tok_rows, width).astype(jnp.bfloat16),
        init_grad,
    )


def solution(mesh):
    return jax.shard_map(
        shards,
        mesh=mesh,
        in_specs=(
            P("seq", "head"),
            P("seq", "head"),
            P("seq", "head"),
            P("head", None, None),
            P(("head", "seq"), None),
            P("seq", None),
        ),
        out_specs=(
            P("seq", "head"),
            P("seq", "head"),
            P("seq", "head"),
            P("seq", "head"),
            P("head", None, None),
        ),
        check_vma=False,
    )
```

profile of v0, /device:TPU:1, one launch (start us, length us, event | category | flops | bytes accessed | tf_op | source)
XLA Modules:
  0.0 504.5 jit_solution(3683059020974468242)
XLA Ops:
  7.2 1.5 copy.55
  8.7 1.4 copy.58
  12.3 1.1 select_convert_fusion.1
  13.5 1.7 copy-done
  15.1 2.3 fusion.7
  17.4 86.1 %all-gather.8.cloned.1.call-done = bf16[192,128,128]{2,1,0:T(8,128)(2,1)} async-done(((bf16[6,128,128]{2,1,0:T(8,128)(2,1)}), bf16[192,128,128]{2,1,0:T(8,128)(2,1)}) %all-gather.8.cloned.1.call-update) | async-done | bytes 6291472 | tf_op jit(solution)/shard_map/all_gather | solution.py:13
  103.6 102.9 %all-gather.6.cloned.1.call-done = bf16[768,6144]{1,0:T(8,128)(2,1)} async-done(((bf16[24,6144]{1,0:T(8,128)(2,1)}), bf16[768,6144]{1,0:T(8,128)(2,1)}) %all-gather.6.cloned.1.call-update) | async-done | bytes 9437200 | tf_op jit(solution)/shard_map/all_gather | solution.py:55
  206.5 9.6 %fusion.8 = f32[512,768]{0,1:T(8,128)S(1)} fusion(bf16[512,6144]{1,0:T(8,128)(2,1)} %param.15, bf16[768,6144]{1,0:T(8,128)(2,1)} %all-gather.6.cloned.1.call-done), kind=kOutput, calls=%fused_computation.27 | convolution fusion | flops 4831838208 | bytes 17301504 | tf_op jit(solution)/shard_map/dot_general | solution.py:57
  216.8 1.4 fusion
  220.9 10.8 %convolution_convert_fusion = bf16[512,6144]{1,0:T(8,128)(2,1)} fusion(bf16[512,768]{0,1:T(8,128)(2,1)} %bitcast.83, bf16[768,6144]{1,0:T(8,128)(2,1)} %all-gather.6.cloned.1.call-done), kind=kOutput, calls=%fused_computation.2 | convolution fusion | flops 4834983936 | bytes 16515072 | tf_op jit(solution)/shard_map/dot_general | solution.py:56
  231.7 2.0 select_convert_fusion
  233.8 1.1 fusion.9
  234.9 1.2 fusion.2
  236.2 2.3 copy.71
  238.5 3.8 fusion.10
  242.2 1.8 fusion.11
  244.0 115.4 %all-reduce.2.cloned.1.call-done = bf16[6,128,128]{1,2,0:T(8,128)(2,1)} async-done(((bf16[6,128,128]{1,2,0:T(8,128)(2,1)}), bf16[6,128,128]{1,2,0:T(8,128)(2,1)}) %all-reduce.2.cloned.1.call-update) | async-done | bytes 196624 | tf_op jit(solution)/shard_map/psum | solution.py:88
  359.4 1.8 copy.74
  361.2 91.8 %all-gather.10.cloned.1.call-done = bf16[192,128,128]{2,1,0:T(8,128)(2,1)} async-done(((bf16[6,128,128]{2,1,0:T(8,128)(2,1)}), bf16[192,128,128]{2,1,0:T(8,128)(2,1)}) %all-gather.10.cloned.1.call-update) | async-done | bytes 6291472 | tf_op jit(solution)/shard_map/all_gather | solution.py:13
  453.0 32.2 %while.23 = (s32[]{:T(128)}, f32[6,128,128]{2,1,0:T(8,128)S(1)}, s32[]{:T(128)}, bf16[32,6,128,128]{3,2,1,0:T(8,128)(2,1)}, s32[]{:T(128)}, /*index=5*/s32[]{:T(128)}, s32[]{:T(128)}, s32[]{:T(128)}) while((s32[]{:T(128)}, f32[6,128,128]{2,1,0:T(8,128)S(1)}, s32[]{:T(128)}, bf16[32,6,128,128]{3,2,1,0:T(8,128)(2,1)}, s32[]{:T(128)}, ...), condition=%wide.region_6.7_spmd, body=%wide.region_5.6_spmd.sunk | while | flops 196614 | bytes 983183 | solution.py:20
  485.3 2.9 add_convert_fusion
  488.1 2.3 copy.73
  490.8 1.2 copy.72
  491.9 6.0 %reduce-scatter.2.cloned.1.call-done = bf16[512,768]{1,0:T(8,128)(2,1)} async-done(((bf16[512,6144]{1,0:T(8,128)(2,1)}), bf16[512,768]{1,0:T(8,128)(2,1)}) %reduce-scatter.2.cloned.1.call-update) | async-done | bytes 786448 | tf_op jit(solution)/shard_map/reduce_scatter | solution.py:60
  (70 shorter events, 37.5 us)
Async XLA Ops:
  7.2 4.8 copy-start.6
  7.2 96.3 %all-gather.8.cloned.1.call-start = ((), (), s32[]{:S(2)}) async-start(), calls=%async_computation.4 | async-start | bytes 6488064 | tf_op jit(solution)/shard_map/all_gather | solution.py:13
  11.2 195.4 %all-gather.6.cloned.1.call-start = ((), (), s32[]{:S(2)}) async-start(), calls=%async_computation.1 | async-start | bytes 9732096 | tf_op jit(solution)/shard_map/all_gather | solution.py:55
  12.3 1.1 copy-start.8
  13.4 1.7 copy-start
  17.4 86.2 %copy-start.7 = (f32[6,128,128]{2,1,0:T(8,128)S(1)}, f32[6,128,128]{2,1,0:T(8,128)}, u32[]{:S(2)}) copy-start(f32[6,128,128]{2,1,0:T(8,128)} %param.13) | copy-start | bytes 1179652
  206.5 9.6 %copy-start.4 = (f32[6,512,128]{1,2,0:T(8,128)S(1)}, f32[6,512,128]{1,2,0:T(8,128)}, u32[]{:S(2)}) copy-start(f32[6,512,128]{1,2,0:T(8,128)} %fusion.7) | copy-start | bytes 4718596
  218.5 0.8 copy-start.5
  219.4 140.0 %all-reduce.2.cloned.1.call-start = ((), (), s32[]{:S(2)}) async-start(), calls=%async_computation.3 | async-start | bytes 393216 | tf_op jit(solution)/shard_map/psum | solution.py:88
  220.1 232.9 %all-gather.10.cloned.1.call-start = ((), (), s32[]{:S(2)}) async-start(), calls=%async_computation.5 | async-start | bytes 6488064 | tf_op jit(solution)/shard_map/all_gather | solution.py:13
  220.7 277.3 %reduce-scatter.2.cloned.1.call-start = ((), (), s32[]{:S(2)}) async-start(), calls=%async_computation.2 | async-start | bytes 7077888 | tf_op jit(solution)/shard_map/reduce_scatter | solution.py:60
  233.8 2.4 copy-start.1
  238.4 3.8 copy-start.2
  485.3 5.2 %copy-start.3 = (f32[6,512,128]{1,2,0:T(8,128)S(1)}, f32[6,512,128]{1,2,0:T(8,128)}, u32[]{:S(2)}) copy-start(f32[6,512,128]{1,2,0:T(8,128)} %fusion.11) | copy-start | bytes 4718596
Sparse Core Ops, SparseCore 0:
  11.3 92.1 all-gather.7
  106.1 100.4 all-gather.5
  223.6 135.7 all-reduce.1
  362.7 90.2 all-gather.9
  456.1 41.7 reduce-scatter.1
where the time goes:
time: 506 us; the launch traced here: 504 us
  waiting for transfers between devices  404 us (80%)
  matrix products  38.9 us (8%)
  other arithmetic  33 us (7%)
  between operations  14 us (3%)
  local copies, waits for them, and re-layouts  13.3 us (3%)
    all_gather x2, waiting for transfers between devices, prefix(): gathered = lax.all_gather(value.astype(jnp.bfloat16), axis)  178 us
    psum x1, waiting for transfers between devices, shards(): lax.psum(own_adjoint.astype(jnp.bfloat16), 'seq').astype(jnp.float32)  115 us
    all_gather x1, waiting for transfers between devices, shards(): weight_rows = lax.all_gather(out_weight, 'seq', axis=0, tiled=True)  103 us
    add x31, other arithmetic, add_states(): return earlier + later  31.5 us
    unnamed x25, local copies, waits for them, and re-layouts  12.4 us
    dot_general x1, matrix products, shards(): projected = jnp.dot(normed, weight_rows, preferred_element_type=jnp.float32)  10.8 us
  transfers between devices with their start and end apart: 5, of which 5 were waited for; matrix products, arithmetic and copies ran while one was open for 13% of the time, Pallas kernels for 0%

commit v1 on v0

--- a/solution.py
+++ b/solution.py
@@ -52,7 +52,9 @@
         "thi,hij->thj", queries, state_half, preferred_element_type=jnp.float32
     )
     normed = normalize(attended).astype(jnp.bfloat16).reshape(tok_rows, width)
-    weight_rows = lax.all_gather(out_weight, "seq", axis=0, tiled=True)
+    weight_rows = jnp.concatenate(
+        lax.all_to_all(jnp.stack([out_weight] * lax.axis_size("seq")), "seq", 0, 0), axis=0
+    )
     projected = jnp.dot(normed, weight_rows, preferred_element_type=jnp.float32)
     grad_normed = lax.dot_general(
         out_grad, weight_rows, (((1,), (1,)), ((), ())), preferred_element_type=jnp.float32

time: 506 us -> 579 us (1.14)
  waiting for transfers between devices: 404 us -> 461 us
  starting transfers between devices: 0.34 us -> 12.6 us
    all_gather x2, waiting for transfers between devices: 178 us -> 291 us  [prefix(): gathered = lax.all_gather(value.astype(jnp.bfloat16), axis)]
    all_gather x1 -> x0, waiting for transfers between devices: 103 us -> none  [shards(): weight_rows = lax.all_gather(out_weight, 'seq', axis=0, tiled=True)]
    all_to_all x0 -> x1, waiting for transfers between devices: none -> 32.5 us  [shards(): lax.all_to_all(jnp.stack([out_weight] * lax.axis_size('seq')), 'seq', 0, 0)]
    psum x1, waiting for transfers between devices: 115 us -> 130 us  [shards(): lax.psum(own_adjoint.astype(jnp.bfloat16), 'seq').astype(jnp.float32)]
    all_to_all x0 -> x1, starting transfers between devices: none -> 12.3 us  [shards(): lax.all_to_all(jnp.stack([out_weight] * lax.axis_size('seq')), 'seq', 0, 0)]
    unnamed x25 -> x27, local copies, waits for them, and re-layouts: 12.4 us -> 11.3 us
  transfers between devices with their start and end apart: 5 -> 5, of which waited for: 5 -> 5; matrix products, arithmetic and copies ran while one was open for 13% -> 12% of each run, Pallas kernels for 0% -> 0%
where the time goes in v1:
time: 579 us; the launch traced here: 578 us
  waiting for transfers between devices  461 us (80%)
  matrix products  39 us (7%)
  other arithmetic  33 us (6%)
  local copies, waits for them, and re-layouts  17.9 us (3%)
  between operations  14 us (2%)
  starting transfers between devices  12.6 us (2%)
    all_gather x2, waiting for transfers between devices, prefix(): gathered = lax.all_gather(value.astype(jnp.bfloat16), axis)  291 us
    psum x1, waiting for transfers between devices, shards(): lax.psum(own_adjoint.astype(jnp.bfloat16), 'seq').astype(jnp.float32)  130 us
    all_to_all x1, waiting for transfers between devices, shards(): lax.all_to_all(jnp.stack([out_weight] * lax.axis_size('seq')), 'seq', 0, 0)  32.5 us
    add x31, other arithmetic, add_states(): return earlier + later  31.5 us
    all_to_all x1, starting transfers between devices, shards(): lax.all_to_all(jnp.stack([out_weight] * lax.axis_size('seq')), 'seq', 0, 0)  12.3 us
  transfers between devices with their start and end apart: 5, of which 5 were waited for; matrix products, arithmetic and copies ran while one was open for 12% of the time, Pallas kernels for 0%

profile of v1, /device:TPU:1, one launch (start us, length us, event | category | flops | bytes accessed | tf_op | source)
XLA Modules:
  0.0 578.2 jit_solution(17032272657107158921)
XLA Ops:
  7.2 5.8 %stack.2 = bf16[32,24,6144]{2,1,0:T(8,128)(2,1)} broadcast(bf16[24,6144]{1,0:T(8,128)(2,1)} %param.14), dimensions={1,2} | broadcast | bytes 9732096 | tf_op jit(solution)/shard_map/stack | solution.py:56
  13.0 12.3 %all-to-all-start = ((bf16[32,24,6144]{2,1,0:T(8,128)(2,1)}), bf16[32,24,6144]{2,1,0:T(8,128)(2,1)}, u32[]{:S(2)}, u32[]{:S(2)}) async-start(bf16[32,24,6144]{2,1,0:T(8,128)(2,1)} %stack.2), calls=%async_computation | async-start | bytes 18874368 | tf_op jit(solution)/shard_map/all_to_all | solution.py:56
  27.0 1.4 copy.52
  29.6 1.7 copy-done
  31.3 2.4 fusion.9
  33.7 198.7 %all-gather.5.cloned.1.call-done = bf16[192,128,128]{2,1,0:T(8,128)(2,1)} async-done(((bf16[6,128,128]{2,1,0:T(8,128)(2,1)}), bf16[192,128,128]{2,1,0:T(8,128)(2,1)}) %all-gather.5.cloned.1.call-update) | async-done | bytes 6291472 | tf_op jit(solution)/shard_map/all_gather | solution.py:13
  232.5 32.5 %all-to-all-done = bf16[32,24,6144]{2,1,0:T(8,128)(2,1)} async-done(((bf16[32,24,6144]{2,1,0:T(8,128)(2,1)}), bf16[32,24,6144]{2,1,0:T(8,128)(2,1)}, u32[]{:S(2)}, u32[]{:S(2)}) %all-to-all-start) | async-done | bytes 9437216 | tf_op jit(solution)/shard_map/all_to_all | solution.py:56
  265.0 9.6 %fusion = f32[512,6,128]{0,2,1:T(8,128)S(1)} fusion(bf16[6,128,6144]{2,1,0:T(8,128)(2,1)} %bitcast.11, bf16[512,6144]{1,0:T(8,128)(2,1)} %param.15), kind=kOutput, calls=%fused_computation.3 | convolution fusion | flops 4831838208 | bytes 17301504 | tf_op jit(solution)/shard_map/dot_general | solution.py:59
  275.3 1.4 fusion.2
  279.5 10.8 %convolution_convert_fusion = bf16[512,6144]{1,0:T(8,128)(2,1)} fusion(bf16[512,768]{0,1:T(8,128)(2,1)} %bitcast.84, bf16[768,6144]{1,0:T(8,128)(2,1)} %bitcast.9), kind=kOutput, calls=%fused_computation.2 | convolution fusion | flops 4834983936 | bytes 16515072 | tf_op jit(solution)/shard_map/dot_general | solution.py:58
  290.4 2.0 select_convert_fusion
  292.4 1.1 fusion.10
  293.6 1.2 fusion.4
  294.8 2.3 copy.68
  297.1 3.8 fusion.12
  300.9 1.7 fusion.11
  302.6 130.3 %all-reduce.2.cloned.1.call-done = bf16[6,128,128]{1,2,0:T(8,128)(2,1)} async-done(((bf16[6,128,128]{1,2,0:T(8,128)(2,1)}), bf16[6,128,128]{1,2,0:T(8,128)(2,1)}) %all-reduce.2.cloned.1.call-update) | async-done | bytes 196624 | tf_op jit(solution)/shard_map/psum | solution.py:90
  432.9 1.8 copy.71
  434.7 92.0 %all-gather.7.cloned.1.call-done = bf16[192,128,128]{2,1,0:T(8,128)(2,1)} async-done(((bf16[6,128,128]{2,1,0:T(8,128)(2,1)}), bf16[192,128,128]{2,1,0:T(8,128)(2,1)}) %all-gather.7.cloned.1.call-update) | async-done | bytes 6291472 | tf_op jit(solution)/shard_map/all_gather | solution.py:13
  526.8 32.2 %while.23 = (s32[]{:T(128)}, f32[6,128,128]{2,1,0:T(8,128)S(1)}, s32[]{:T(128)}, bf16[32,6,128,128]{3,2,1,0:T(8,128)(2,1)}, s32[]{:T(128)}, /*index=5*/s32[]{:T(128)}, s32[]{:T(128)}, s32[]{:T(128)}) while((s32[]{:T(128)}, f32[6,128,128]{2,1,0:T(8,128)S(1)}, s32[]{:T(128)}, bf16[32,6,128,128]{3,2,1,0:T(8,128)(2,1)}, s32[]{:T(128)}, ...), condition=%wide.region_6.7_spmd, body=%wide.region_5.6_spmd.sunk | while | flops 196614 | bytes 983183 | solution.py:20
  559.0 2.8 fusion.3
  561.8 2.3 copy.69
  564.5 1.2 copy.70
  565.7 6.0 %reduce-scatter.2.cloned.1.call-done = bf16[512,768]{1,0:T(8,128)(2,1)} async-done(((bf16[512,6144]{1,0:T(8,128)(2,1)}), bf16[512,768]{1,0:T(8,128)(2,1)}) %reduce-scatter.2.cloned.1.call-update) | async-done | bytes 786448 | tf_op jit(solution)/shard_map/reduce_scatter | solution.py:62
  (72 shorter events, 38.3 us)
Async XLA Ops:
  13.0 12.3 %copy-start.6 = (bf16[512,768]{1,0:T(8,128)(2,1)S(1)}, bf16[512,768]{1,0:T(8,128)(2,1)}, u32[]{:S(2)}) copy-start(bf16[512,768]{1,0:T(8,128)(2,1)} %param.11) | copy-start | bytes 2359300
  13.0 12.6 %copy-start.7 = (bf16[512,768]{1,0:T(8,128)(2,1)S(1)}, bf16[512,768]{1,0:T(8,128)(2,1)}, u32[]{:S(2)}) copy-start(bf16[512,768]{1,0:T(8,128)(2,1)} %param.12) | copy-start | bytes 2359300
  13.0 252.1 %all-to-all-start = ((bf16[32,24,6144]{2,1,0:T(8,128)(2,1)}), bf16[32,24,6144]{2,1,0:T(8,128)(2,1)}, u32[]{:S(2)}, u32[]{:S(2)}) async-start(bf16[32,24,6144]{2,1,0:T(8,128)(2,1)} %stack.2), calls=%async_computation | async-start | bytes 18874368 | tf_op jit(solution)/shard_map/all_to_all | solution.py:56
  25.2 207.1 %all-gather.5.cloned.1.call-start = ((), (), s32[]{:S(2)}) async-start(), calls=%async_computation.4 | async-start | bytes 6488064 | tf_op jit(solution)/shard_map/all_gather | solution.py:13
  28.5 1.1 copy-start.9
  29.6 1.7 copy-start
  33.7 198.7 %copy-start.8 = (f32[6,128,128]{2,1,0:T(8,128)S(1)}, f32[6,128,128]{2,1,0:T(8,128)}, u32[]{:S(2)}) copy-start(f32[6,128,128]{2,1,0:T(8,128)} %param.13) | copy-start | bytes 1179652
  265.0 9.6 %copy-start.4 = (f32[6,512,128]{1,2,0:T(8,128)S(1)}, f32[6,512,128]{1,2,0:T(8,128)}, u32[]{:S(2)}) copy-start(f32[6,512,128]{1,2,0:T(8,128)} %fusion.9) | copy-start | bytes 4718596
  277.0 0.8 copy-start.5
  277.8 155.1 %all-reduce.2.cloned.1.call-start = ((), (), s32[]{:S(2)}) async-start(), calls=%async_computation.3 | async-start | bytes 393216 | tf_op jit(solution)/shard_map/psum | solution.py:90
  278.6 248.2 %all-gather.7.cloned.1.call-start = ((), (), s32[]{:S(2)}) async-start(), calls=%async_computation.5 | async-start | bytes 6488064 | tf_op jit(solution)/shard_map/all_gather | solution.py:13
  279.3 292.4 %reduce-scatter.2.cloned.1.call-start = ((), (), s32[]{:S(2)}) async-start(), calls=%async_computation.2 | async-start | bytes 7077888 | tf_op jit(solution)/shard_map/reduce_scatter | solution.py:62
  292.4 2.4 copy-start.2
  297.1 3.8 copy-start.1
  559.0 5.1 copy-start.3
Sparse Core Ops, SparseCore 0:
  29.2 203.0 all-gather.4
  282.1 150.8 all-reduce.1
  436.4 90.2 all-gather.6
  529.9 41.7 reduce-scatter.1
